TPU v7x, 256 devices: a whole 4x4x8 slice. The times are simulated.
256 devices in a mesh: dp: 16 (over x_hi, y, core), seq: 16 (over z, x_lo).
Axes of the slice: x: 4 (x_hi: 2, x_lo: 2; x = x_hi * 2 + x_lo), y: 4, z: 8, core: 2. Of those that a mesh axis runs over, the one named last changes fastest.
Arguments:
- layer_input: bfloat16 [16, 2048, 5120], P('dp', 'seq'), may hold values from -6 to 6
- query_states: bfloat16 [16, 2048, 2560], P('dp', 'seq'), may hold values from -24 to 24
- key_states: bfloat16 [16, 2048, 512], P('dp', 'seq'), may hold values from -6 to 6
- out_grad: bfloat16 [16, 2048, 2560], P('dp', 'seq'), may hold values from -12 to 12
- value_weight: bfloat16 [5120, 512], P('dp'), may hold values from -0.078125 to 0.078125
- segment_ids: int32 [16, 2048], P('dp'), may hold values from 0 to 31, as said below
- pair_split: int32 [16, 32], P('dp'), may hold values from 1 to 2047, as said below
Outputs:
- query_grad: bfloat16 [16, 2048, 2560], P('dp', 'seq')
- key_grad: bfloat16 [16, 2048, 512], P('dp', 'seq')
- input_grad: bfloat16 [16, 2048, 5120], P('dp', 'seq')
- weight_grad: float32 [5120, 512], P('dp', 'seq')
Inputs may be any that keep to these rules, and one draw needn't show every extreme that they name: `segment_ids`: each packed row holds 32 sentence pairs numbered 0 to 31 in order along the row; each pair has 16 to 112 positions, every row has a pair of exactly 112, and the pair lengths of a row can be matched two by two into sums of 128. pair_split[r, s] lies after the first position of pair s and at or before its last position; in every row the first pair's second sentence begins at position 1 and the last pair's at position 2047.
All inputs are finite; a program needn't handle non-finite values.
Results may differ from a plain program's by a relative error of at most 0.0057.
Values may be sent and summed in bfloat16 or wider, within the bound.
A program may use at most 128 MiB of HBM per device.

v0:
```python
import jax
import jax.numpy as jnp
from jax import lax
from jax.sharding import PartitionSpec as P

HD = 128


def with_halo(cells, sides, width):
    for axis, dim in sides:
        count = lax.axis_size(axis)
        ends = count - 1
        head = lax.slice_in_dim(cells, 0, width, axis=dim)
        tail = lax.slice_in_dim(cells, cells.shape[dim] - width, cells.shape[dim], axis=dim)
        cells = jnp.concatenate(
            [
                lax.ppermute(tail, axis, [(i, (i + 1) % count) for i in range(ends)]),
                cells,
                lax.ppermute(head, axis, [((i + 1) % count, i) for i in range(ends)]),
            ],
            axis=dim,
        )
    return cells


def passed_along(array, axis, by):
    count = lax.axis_size(axis)
    pairs = [(i, i + by) for i in range(count) if 0 <= i + by < count]
    return lax.ppermute(array, axis, pairs)


def attend_block(query_rows, key_rows, value_rows, grad_rows, visible):
    rows_here = query_rows.shape[0]
    keys_here = key_rows.shape[0]
    head_count = key_rows.shape[1] // HD
    group_size = query_rows.shape[1] // key_rows.shape[1]
    score_scale = HD ** (-0.5)
    high = lax.Precision.HIGHEST
    query_split = query_rows.reshape(rows_here, head_count, group_size, HD)
    grad_split = grad_rows.reshape(rows_here, head_count, group_size, HD)
    key_split = key_rows.reshape(keys_here, head_count, HD)
    value_split = value_rows.reshape(keys_here, head_count, HD)
    query_parts = []
    key_parts = []
    value_parts = []
    for kv_group in range(head_count):
        query_head = query_split[:, kv_group]
        grad_head = grad_split[:, kv_group]
        key_head = key_split[:, kv_group]
        value_head = value_split[:, kv_group]
        scores = (
            jnp.einsum("qgd,kd->gqk", query_head, key_head, preferred_element_type=jnp.float32)
            * score_scale
        )
        masked = jnp.where(visible[None], scores, -1e30)
        highest = jnp.max(masked, axis=-1, keepdims=True)
        weights = jnp.where(visible[None], jnp.exp(masked - highest), 0.0)
        attention = weights / jnp.sum(weights, axis=-1, keepdims=True)
        attention_low = attention.astype(jnp.bfloat16)
        prob_grad = jnp.einsum(
            "qgd,kd->gqk", grad_head, value_head, preferred_element_type=jnp.float32
        )
        row_delta = jnp.sum(attention * prob_grad, axis=-1, keepdims=True)
        score_grad = attention * (prob_grad - row_delta)
        key_wide = key_head.astype(jnp.float32)
        query_wide = query_head.astype(jnp.float32)
        query_parts.append(
            jnp.einsum("gqk,kd->qgd", score_grad, key_wide, precision=high) * score_scale
        )
        key_parts.append(
            jnp.einsum("gqk,qgd->kd", score_grad, query_wide, precision=high) * score_scale
        )
        value_parts.append(
            jnp.einsum("gqk,qgd->kd", attention_low, grad_head, preferred_element_type=jnp.float32)
        )
    query_grad = jnp.stack(query_parts, axis=1).reshape(rows_here, -1)
    kv_grad = jnp.concatenate(key_parts + value_parts, axis=1)
    return (query_grad, kv_grad)


def local(layer_input, query_states, key_states, out_grad, value_weight, segment_ids, pair_split):
    layer_rows = layer_input[0]
    tok_count = layer_rows.shape[0]
    kv_width = key_states.shape[2]
    row_base = lax.axis_index("seq") * tok_count
    columns = layer_rows
    value_rows = jnp.dot(
        columns,
        lax.all_gather(value_weight, "dp", axis=0, tiled=True),
        preferred_element_type=jnp.float32,
    )
    value_low = value_rows.astype(jnp.bfloat16)
    both_states = jnp.concatenate([key_states[0], value_low], axis=1)
    extended = with_halo(both_states, (("seq", 0),), tok_count)
    key_block = extended[:, :kv_width]
    value_block = extended[:, kv_width:]
    seg_row = segment_ids[0]
    fill_ids = jnp.full((tok_count,), -1, jnp.int32)
    padded_ids = jnp.concatenate([fill_ids, seg_row, fill_ids])
    seg_key = lax.dynamic_slice_in_dim(padded_ids, row_base, tok_count + 2 * tok_count, 0)
    seg_query = lax.dynamic_slice_in_dim(seg_row, row_base, tok_count, 0)
    pair_numbers = jnp.arange(pair_split.shape[1], dtype=jnp.int32)
    split_query = jnp.sum(
        jnp.where(seg_query[:, None] == pair_numbers[None, :], pair_split[0][None, :], 0), axis=1
    )
    pos_query = row_base + jnp.arange(tok_count, dtype=jnp.int32)
    pos_key = row_base - tok_count + jnp.arange(tok_count + 2 * tok_count, dtype=jnp.int32)
    visible = (seg_key[None, :] == seg_query[:, None]) & (
        (pos_key[None, :] <= pos_query[:, None]) | (pos_key[None, :] < split_query[:, None])
    )
    query_grad, kv_grad = attend_block(
        query_states[0], key_block, value_block, out_grad[0], visible
    )
    lower_rim = kv_grad[:tok_count]
    upper_rim = kv_grad[tok_count + tok_count :]
    center = kv_grad[tok_count : tok_count + tok_count]
    from_upper = passed_along(lower_rim, "seq", -1)
    from_lower = passed_along(upper_rim, "seq", 1)
    center = center + from_upper + from_lower
    key_grad = center[:, :kv_width].astype(jnp.bfloat16)
    value_grad = center[:, kv_width:].astype(jnp.bfloat16)
    input_grad = lax.dot_general(
        value_grad,
        lax.all_gather(value_weight, "dp", axis=0, tiled=True),
        (((1,), (1,)), ((), ())),
        preferred_element_type=jnp.float32,
    )
    dp_count = lax.axis_size("dp")
    model_width = layer_rows.shape[1]
    input_blocks = lax.all_to_all(
        layer_rows.reshape(tok_count, dp_count, model_width // dp_count).transpose(1, 0, 2),
        "dp",
        0,
        0,
        tiled=True,
    )
    grad_rows = lax.all_gather(value_grad, "dp", axis=0, tiled=False)
    own_rows = jnp.einsum(
        "rtk,rtc->kc", input_blocks, grad_rows, preferred_element_type=jnp.float32
    )
    summed = lax.psum_scatter(own_rows, "seq", scatter_dimension=1, tiled=True)
    devices_all = lax.axis_size("dp") * lax.axis_size("seq")
    weight_grad = summed / devices_all
    return (
        query_grad.astype(jnp.bfloat16)[None],
        key_grad[None],
        input_grad.astype(jnp.bfloat16)[None],
        weight_grad,
    )


def solution(mesh):
    return jax.shard_map(
        local,
        mesh=mesh,
        in_specs=(
            P("dp", "seq", None),
            P("dp", "seq", None),
            P("dp", "seq", None),
            P("dp", "seq", None),
            P("dp", None),
            P("dp", None),
            P("dp", None),
        ),
        out_specs=(
            P("dp", "seq", None),
            P("dp", "seq", None),
            P("dp", "seq", None),
            P("dp", "seq"),
        ),
        check_vma=False,
    )
```

profile of v0, /device:TPU:8, one launch (start us, length us, event | category | flops | bytes accessed | tf_op | source)
XLA Modules:
  0.0 293.2 jit_solution(11749638976114022956)
XLA Ops:
  7.2 0.7 all-gather.4.cloned.1.call-update
  7.9 0.7 dynamic-slice_bitcast_fusion
  8.6 0.8 fusion.57
  9.4 0.7 select_reduce_fusion
  10.1 67.0 %all-gather.4.cloned.1.call-done = bf16[5120,512]{1,0:T(8,128)(2,1)} async-done(((bf16[320,512]{1,0:T(8,128)(2,1)}), bf16[5120,512]{1,0:T(8,128)(2,1)}) %all-gather.4.cloned.1.call-update) | async-done | bytes 5242896 | tf_op jit(solution)/shard_map/all_gather | solution.py:89
  77.2 3.7 %fusion.35 = bf16[128,512]{1,0:T(8,128)(2,1)S(1)} fusion(bf16[5120,512]{1,0:T(8,128)(2,1)} %all-gather.4.cloned.1.call-done, bf16[1,128,5120]{2,1,0:T(8,128)(2,1)} %param.7), kind=kOutput, calls=%fused_computation.53 | convolution fusion | flops 671154176 | bytes 6684672 | tf_op jit(solution)/shard_map/dot_general | solution.py:87
  81.0 1.4 collective-permute-start.1
  82.4 5.3 %collective-permute-start = (bf16[128,1024]{1,0:T(8,128)(2,1)S(1)}, bf16[128,1024]{1,0:T(8,128)(2,1)}, u32[]{:S(2)}, u32[]{:S(2)}) collective-permute-start(bf16[128,1024]{1,0:T(8,128)(2,1)S(1)} %pad_maximum_fusion.2), channel_id=1, source_target_pairs={{0,1},{1,2},{2,3},{3,4},{4,5},{5,6},{6,7},{7,8},{8,9},{9,10},{10,1... | collective-permute-start | bytes 786440 | tf_op jit(solution)/shard_map/ppermute | solution.py:17
  88.6 2.9 collective-permute-done.1
  91.5 4.6 %collective-permute-done = bf16[128,1024]{1,0:T(8,128)(2,1)} collective-permute-done((bf16[128,1024]{1,0:T(8,128)(2,1)S(1)}, bf16[128,1024]{1,0:T(8,128)(2,1)}, u32[]{:S(2)}, u32[]{:S(2)}) %collective-permute-start) | collective-permute-done | bytes 262176 | tf_op jit(solution)/shard_map/ppermute | solution.py:17
  96.1 1.0 pad_maximum_fusion
  97.4 1.4 fusion.74
  98.8 0.6 fusion.73
  99.4 1.5 fusion.79
  100.8 1.4 fusion.78
  102.3 1.4 fusion.77
  103.7 1.5 fusion.76
  105.3 1.6 multiply_reduce_fusion.3
  107.0 0.7 fusion.45
  109.0 0.8 fusion.43
  111.0 0.7 fusion.41
  112.9 1.0 copy-done.29
  114.0 0.8 fusion.39
  114.7 1.7 fusion.34
  116.4 1.7 fusion.33
  118.1 1.6 fusion.32
  119.7 1.6 fusion.31
  121.4 1.4 collective-permute-start.2
  122.9 5.1 %collective-permute-start.3 = (f32[128,1024]{0,1:T(8,128)S(1)}, f32[128,1024]{0,1:T(8,128)S(1)}, u32[]{:S(2)}, u32[]{:S(2)}) collective-permute-start(f32[128,1024]{0,1:T(8,128)S(1)} %get-tuple-element.21), channel_id=1, source_target_pairs={{0,1},{1,2},{2,3},{3,4},{4,5},{5,6},{6,7},{7,8},{8,9},{9,10},{10,1... | collective-permute-start | bytes 1572872 | tf_op jit(solution)/shard_map/ppermute | solution.py:29
  128.0 10.1 %collective-permute-done.2 = f32[128,1024]{0,1:T(8,128)S(1)} collective-permute-done((f32[128,1024]{0,1:T(8,128)S(1)}, f32[128,1024]{0,1:T(8,128)S(1)}, u32[]{:S(2)}, u32[]{:S(2)}) %collective-permute-start.2) | collective-permute-done | bytes 524320 | tf_op jit(solution)/shard_map/ppermute | solution.py:29
  138.2 11.4 %collective-permute-done.3 = f32[128,1024]{0,1:T(8,128)S(1)} collective-permute-done((f32[128,1024]{0,1:T(8,128)S(1)}, f32[128,1024]{0,1:T(8,128)S(1)}, u32[]{:S(2)}, u32[]{:S(2)}) %collective-permute-start.3) | collective-permute-done | bytes 524320 | tf_op jit(solution)/shard_map/ppermute | solution.py:29
  149.6 0.7 fusion.75
  150.3 1.4 copy.184
  151.8 6.2 %all-to-all-start = ((bf16[16,128,320]{1,2,0:T(8,128)(2,1)}), bf16[16,128,320]{1,2,0:T(8,128)(2,1)}, u32[]{:S(2)}, u32[]{:S(2)}) async-start(bf16[16,128,320]{1,2,0:T(8,128)(2,1)} %bitcast.64), calls=%async_computation | async-start | bytes 2621440 | tf_op jit(solution)/shard_map/all_to_all | solution.py:130
  158.1 50.0 %all-gather.6.cloned.1.call-done = bf16[2048,512]{0,1:T(8,128)(2,1)} async-done(((bf16[128,512]{0,1:T(8,128)(2,1)}), bf16[2048,512]{0,1:T(8,128)(2,1)}) %all-gather.6.cloned.1.call-update) | async-done | bytes 2097168 | tf_op jit(solution)/shard_map/all_gather | solution.py:137
  208.1 2.9 copy.217
  211.0 2.1 convolution_bitcast_fusion.4
  213.2 1.2 copy.218
  214.7 2.0 fusion.49
  216.8 0.7 fusion.48
  218.3 0.7 fusion.47
  219.8 0.7 fusion.46
  220.5 1.1 copy.186
  221.6 0.8 copy.187
  222.4 5.4 %fusion.4 = bf16[1,128,5120]{2,1,0:T(8,128)(2,1)} fusion(bf16[5120,512]{1,0:T(8,128)(2,1)} %all-gather.4.cloned.1.call-done, bf16[128,1024]{0,1:T(8,128)(2,1)S(1)} %fusion.51), kind=kOutput, calls=%fused_computation.5 | convolution fusion | flops 671744000 | bytes 6684672 | tf_op jit(solution)/shard_map/dot_general | solution.py:122
  227.8 57.3 %reduce-scatter.4.cloned.1.call-done = f32[32,320]{1,0:T(8,128)} async-done(((f32[512,320]{1,0:T(8,128)}), f32[32,320]{1,0:T(8,128)}) %reduce-scatter.4.cloned.1.call-update) | async-done | bytes 40976
  285.0 0.9 copy.219
  286.0 0.7 copy.188
  (99 shorter events, 7.1 us)
Async XLA Ops:
  7.2 70.0 %all-gather.4.cloned.1.call-start = ((), (), s32[]{:S(2)}) async-start(), calls=%async_computation.2 | async-start | bytes 5570560 | tf_op jit(solution)/shard_map/all_gather | solution.py:89
  7.9 200.2 %all-gather.6.cloned.1.call-start = ((), (), s32[]{:S(2)}) async-start(), calls=%async_computation.3 | async-start | bytes 2228224 | tf_op jit(solution)/shard_map/all_gather | solution.py:137
  10.1 70.8 %copy-start.7 = (bf16[1,128,512]{2,1,0:T(8,128)(2,1)S(1)}, bf16[1,128,512]{2,1,0:T(8,128)(2,1)}, u32[]{:S(2)}) copy-start(bf16[1,128,512]{2,1,0:T(8,128)(2,1)} %param.9) | copy-start | bytes 393220
  10.1 77.6 %copy-start.1 = (bf16[1,128,2560]{2,1,0:T(8,128)(2,1)S(1)}, bf16[1,128,2560]{2,1,0:T(8,128)(2,1)}, u32[]{:S(2)}) copy-start(bf16[1,128,2560]{2,1,0:T(8,128)(2,1)} %param.8) | copy-start | bytes 1966084
  80.9 7.1 %copy-start.2 = (bf16[1,128,2560]{2,1,0:T(8,128)(2,1)S(1)}, bf16[1,128,2560]{2,1,0:T(8,128)(2,1)}, u32[]{:S(2)}) copy-start(bf16[1,128,2560]{2,1,0:T(8,128)(2,1)} %param.10) | copy-start | bytes 1966084
  81.0 10.5 %collective-permute-start.1 = (bf16[128,1024]{1,0:T(8,128)(2,1)S(1)}, bf16[128,1024]{1,0:T(8,128)(2,1)S(1)}, u32[]{:S(2)}, u32[]{:S(2)}) collective-permute-start(bf16[128,1024]{1,0:T(8,128)(2,1)S(1)} %pad_maximum_fusion.2), channel_id=1, source_target_pairs={{1,0},{2,1},{3,2},{4,3},{5,4},{6,5},{7,6},{8,7},{9,8},{10,9},{11,1... | collective-permute-start | bytes 786440 | tf_op jit(solution)/shard_map/ppermute | solution.py:19
  82.4 13.7 %collective-permute-start = (bf16[128,1024]{1,0:T(8,128)(2,1)S(1)}, bf16[128,1024]{1,0:T(8,128)(2,1)}, u32[]{:S(2)}, u32[]{:S(2)}) collective-permute-start(bf16[128,1024]{1,0:T(8,128)(2,1)S(1)} %pad_maximum_fusion.2), channel_id=1, source_target_pairs={{0,1},{1,2},{2,3},{3,4},{4,5},{5,6},{6,7},{7,8},{8,9},{9,10},{10,1... | collective-permute-start | bytes 786440 | tf_op jit(solution)/shard_map/ppermute | solution.py:17
  88.0 15.7 %copy-start.3 = (bf16[1,128,2560]{1,2,0:T(8,128)(2,1)}, bf16[1,128,2560]{1,2,0:T(8,128)(2,1)S(1)}, u32[]{:S(2)}) copy-start(bf16[1,128,2560]{1,2,0:T(8,128)(2,1)S(1)} %copy.143) | copy-start | bytes 1966084
  88.4 16.9 %copy-start.5 = (bf16[1,128,2560]{1,2,0:T(8,128)(2,1)}, bf16[1,128,2560]{1,2,0:T(8,128)(2,1)S(1)}, u32[]{:S(2)}) copy-start(bf16[1,128,2560]{1,2,0:T(8,128)(2,1)S(1)} %copy.146) | copy-start | bytes 1966084
  88.6 15.1 %copy-start.15 = (pred[128,384]{0,1:T(8,128)(4,1)}, pred[128,384]{0,1:T(8,128)(4,1)S(1)}, u32[]{:S(2)}) copy-start(pred[128,384]{0,1:T(8,128)(4,1)S(1)} %or_and_fusion) | copy-start | bytes 147460
  99.3 2.9 copy-start.8
  99.4 2.9 copy-start.10
  105.3 1.6 copy-start.4
  105.3 1.7 copy-start.22
  106.9 1.0 copy-start.24
  106.9 1.0 copy-start.31
  107.0 1.4 copy-start.6
  107.0 1.4 copy-start.14
  107.0 1.8 copy-start.20
  109.0 1.0 copy-start.25
  109.0 1.0 copy-start.33
  109.0 1.2 copy-start.13
  109.0 1.6 copy-start.18
  111.0 1.0 copy-start.27
  111.0 1.0 copy-start.35
  111.0 1.2 copy-start.12
  111.0 1.6 copy-start.16
  112.9 1.0 copy-start.29
  112.9 1.8 copy-start.37
  121.4 28.9 %copy-start = (bf16[1,128,5120]{2,1,0:T(8,128)(2,1)S(1)}, bf16[1,128,5120]{2,1,0:T(8,128)(2,1)}, u32[]{:S(2)}) copy-start(bf16[1,128,5120]{2,1,0:T(8,128)(2,1)} %param.7) | copy-start | bytes 3932164
  121.4 16.7 %collective-permute-start.2 = (f32[128,1024]{0,1:T(8,128)S(1)}, f32[128,1024]{0,1:T(8,128)S(1)}, u32[]{:S(2)}, u32[]{:S(2)}) collective-permute-start(f32[128,1024]{0,1:T(8,128)S(1)} %get-tuple-element.20), channel_id=1, source_target_pairs={{1,0},{2,1},{3,2},{4,3},{5,4},{6,5},{7,6},{8,7},{9,8},{10,9},{11,1... | collective-permute-start | bytes 1572872 | tf_op jit(solution)/shard_map/ppermute | solution.py:29
  122.9 26.7 %collective-permute-start.3 = (f32[128,1024]{0,1:T(8,128)S(1)}, f32[128,1024]{0,1:T(8,128)S(1)}, u32[]{:S(2)}, u32[]{:S(2)}) collective-permute-start(f32[128,1024]{0,1:T(8,128)S(1)} %get-tuple-element.21), channel_id=1, source_target_pairs={{0,1},{1,2},{2,3},{3,4},{4,5},{5,6},{6,7},{7,8},{8,9},{9,10},{10,1... | collective-permute-start | bytes 1572872 | tf_op jit(solution)/shard_map/ppermute | solution.py:29
  151.8 59.2 %all-to-all-start = ((bf16[16,128,320]{1,2,0:T(8,128)(2,1)}), bf16[16,128,320]{1,2,0:T(8,128)(2,1)}, u32[]{:S(2)}, u32[]{:S(2)}) async-start(bf16[16,128,320]{1,2,0:T(8,128)(2,1)} %bitcast.64), calls=%async_computation | async-start | bytes 2621440 | tf_op jit(solution)/shard_map/all_to_all | solution.py:130
  158.0 127.0 %reduce-scatter.4.cloned.1.call-start = ((), (), s32[]{:S(2)}) async-start(), calls=%async_computation.4 | async-start | bytes 835584
  213.1 1.3 copy-start.11
  213.2 1.5 copy-start.23
  213.2 1.5 copy-start.32
  214.7 2.1 copy-start.9
  214.7 2.1 copy-start.21
  214.7 2.1 copy-start.26
  214.7 2.1 copy-start.34
  216.7 1.2 copy-start.19
  216.8 1.5 copy-start.28
  216.8 1.5 copy-start.36
  218.2 1.2 copy-start.17
  218.3 1.5 copy-start.30
  218.3 1.5 copy-start.38
Sparse Core Ops, SparseCore 0:
  10.8 66.3 all-gather.3
  150.5 57.6 all-gather.5
  214.5 70.4 reduce-scatter.3
where the time goes:
time: 294 us; the launch traced here: 293 us
  waiting for transfers between devices  204 us (69%)
  matrix products  33.3 us (11%)
  starting transfers between devices  19.6 us (7%)
  local copies, waits for them, and re-layouts  19 us (6%)
  between operations  14.3 us (5%)
    all_gather x1, waiting for transfers between devices, local(): lax.all_gather(value_weight, 'dp', axis=0, tiled=True)  67 us
    unnamed x4, waiting for transfers between devices  58 us
    all_gather x1, waiting for transfers between devices, local(): grad_rows = lax.all_gather(value_grad, 'dp', axis=0, tiled=False)  50 us
    ppermute x2, waiting for transfers between devices, passed_along(): return lax.ppermute(array, axis, pairs)  21.5 us
    unnamed x86, local copies, waits for them, and re-layouts  12.5 us
    dot_general x4, matrix products, attend_block(): jnp.einsum('gqk,qgd->kd', attention_low, grad_head, preferred_element_typ...  6.62 us
    ppermute x2, starting transfers between devices, passed_along(): return lax.ppermute(array, axis, pairs)  6.57 us
    all_to_all x1, starting transfers between devices, local(): lax.all_to_all(layer_rows.reshape(tok_count, dp_count, model_width // dp_...  6.25 us
  transfers between devices with their start and end apart: 8, of which 7 were waited for; matrix products, arithmetic and copies ran while one was open for 6% of the time, Pallas kernels for 0%

commit v1 on v0

--- a/solution.py
+++ b/solution.py
@@ -4,6 +4,13 @@
 from jax.sharding import PartitionSpec as P
 
 HD = 128
+
+
+def end_the_domain(panel, along_axis, d_out):
+    known = lax.psum(1, axis_name=along_axis)
+    current_arr = jnp.stack(known * [panel])
+    even = lax.all_to_all(current_arr, axis_name=along_axis, split_axis=0, concat_axis=0)
+    return jnp.concatenate(even, axis=d_out)
 
 
 def with_halo(cells, sides, width):
@@ -85,9 +92,7 @@
     row_base = lax.axis_index("seq") * tok_count
     columns = layer_rows
     value_rows = jnp.dot(
-        columns,
-        lax.all_gather(value_weight, "dp", axis=0, tiled=True),
-        preferred_element_type=jnp.float32,
+        columns, end_the_domain(value_weight, "dp", 0), preferred_element_type=jnp.float32
     )
     value_low = value_rows.astype(jnp.bfloat16)
     both_states = jnp.concatenate([key_states[0], value_low], axis=1)

time: 294 us -> 380 us (1.29)
  waiting for transfers between devices: 204 us -> 273 us
  starting transfers between devices: 19.6 us -> 29.3 us
  local copies, waits for them, and re-layouts: 19 us -> 25.3 us
    all_to_all x0 -> x1, waiting for transfers between devices: none -> 75.7 us  [end_the_domain(): lax.all_to_all(current_arr, axis_name=along_axis, split_axis=0, concat_ax...]
    all_gather x1, waiting for transfers between devices: 67 us -> 50.9 us  [local(): lax.all_gather(value_weight, 'dp', axis=0, tiled=True)]
    unnamed x4, waiting for transfers between devices: 58 us -> 68 us
    all_to_all x0 -> x1, starting transfers between devices: none -> 7.52 us  [end_the_domain(): lax.all_to_all(current_arr, axis_name=along_axis, split_axis=0, concat_ax...]
    another operation x0 -> x1, local copies, waits for them, and re-layouts: none -> 3.85 us  [end_the_domain(): current_arr = jnp.stack(known * [panel])]
    unnamed x86 -> x96, local copies, waits for them, and re-layouts: 12.5 us -> 14.9 us
  transfers between devices with their start and end apart: 8 -> 9, of which waited for: 7 -> 7; matrix products, arithmetic and copies ran while one was open for 6% -> 6% of each run, Pallas kernels for 0% -> 0%
where the time goes in v1:
time: 380 us; the launch traced here: 379 us
  waiting for transfers between devices  273 us (72%)
  matrix products  33.1 us (9%)
  starting transfers between devices  29.3 us (8%)
  local copies, waits for them, and re-layouts  25.3 us (7%)
  between operations  14.3 us (4%)
  other arithmetic  4.13 us (1%)
    all_to_all x1, waiting for transfers between devices, end_the_domain(): lax.all_to_all(current_arr, axis_name=along_axis, split_axis=0, concat_ax...  75.7 us
    unnamed x4, waiting for transfers between devices  68 us
    all_gather x1, waiting for transfers between devices, local(): grad_rows = lax.all_gather(value_grad, 'dp', axis=0, tiled=False)  52.2 us
    all_gather x1, waiting for transfers between devices, local(): lax.all_gather(value_weight, 'dp', axis=0, tiled=True)  50.9 us
    ppermute x2, waiting for transfers between devices, passed_along(): return lax.ppermute(array, axis, pairs)  21.3 us
    unnamed x96, local copies, waits for them, and re-layouts  14.9 us
    all_to_all x1, starting transfers between devices, local(): lax.all_to_all(layer_rows.reshape(tok_count, dp_count, model_width // dp_...  9.2 us
  transfers between devices with their start and end apart: 9, of which 7 were waited for; matrix products, arithmetic and copies ran while one was open for 6% of the time, Pallas kernels for 0%

profile of v1, /device:TPU:8, one launch (start us, length us, event | category | flops | bytes accessed | tf_op | source)
XLA Modules:
  0.0 379.1 jit_solution(13043934268772846819)
XLA Ops:
  7.2 3.8 %stack.17 = bf16[16,320,512]{2,1,0:T(8,128)(2,1)} broadcast(bf16[320,512]{1,0:T(8,128)(2,1)} %param.11), dimensions={1,2} | broadcast | bytes 5570560 | tf_op jit(solution)/shard_map/stack | solution.py:11
  11.0 7.5 %all-to-all-start = ((bf16[16,320,512]{2,1,0:T(8,128)(2,1)}), bf16[16,320,512]{2,1,0:T(8,128)(2,1)}, u32[]{:S(2)}, u32[]{:S(2)}) async-start(bf16[16,320,512]{2,1,0:T(8,128)(2,1)} %stack.17), calls=%async_computation | async-start | bytes 10485760 | tf_op jit(solution)/shard_map/all_to_all | solution.py:12
  18.8 75.7 %all-to-all-done = bf16[16,320,512]{2,1,0:T(8,128)(2,1)} async-done(((bf16[16,320,512]{2,1,0:T(8,128)(2,1)}), bf16[16,320,512]{2,1,0:T(8,128)(2,1)}, u32[]{:S(2)}, u32[]{:S(2)}) %all-to-all-start) | async-done | bytes 5242912 | tf_op jit(solution)/shard_map/all_to_all | solution.py:12
  94.6 3.4 fusion.35
  98.0 0.7 pad_maximum_fusion.2
  98.7 1.3 collective-permute-start.1
  100.0 5.2 %collective-permute-start = (bf16[128,1024]{1,0:T(8,128)(2,1)}, bf16[128,1024]{1,0:T(8,128)(2,1)}, u32[]{:S(2)}, u32[]{:S(2)}) collective-permute-start(bf16[128,1024]{1,0:T(8,128)(2,1)} %pad_maximum_fusion.2), channel_id=1, source_target_pairs={{0,1},{1,2},{2,3},{3,4},{4,5},{5,6},{6,7},{7,8},{8,9},{9,10},{10,1... | collective-permute-start | bytes 786440 | tf_op jit(solution)/shard_map/ppermute | solution.py:24
  106.1 1.1 copy.146
  107.2 1.4 or_and_fusion
  108.8 4.8 %collective-permute-done = bf16[128,1024]{1,0:T(8,128)(2,1)} collective-permute-done((bf16[128,1024]{1,0:T(8,128)(2,1)}, bf16[128,1024]{1,0:T(8,128)(2,1)}, u32[]{:S(2)}, u32[]{:S(2)}) %collective-permute-start) | collective-permute-done | bytes 262176 | tf_op jit(solution)/shard_map/ppermute | solution.py:24
  113.6 1.1 pad_maximum_fusion
  114.8 1.3 fusion.73
  116.2 1.4 fusion.74
  117.6 1.4 fusion.76
  119.1 1.4 fusion.77
  120.5 1.4 fusion.78
  121.9 1.5 fusion.79
  123.4 1.6 multiply_reduce_fusion.3
  125.2 0.8 fusion.45
  130.3 0.7 fusion.43
  131.3 0.7 fusion.41
  132.0 0.8 fusion.39
  132.8 1.8 fusion.34
  134.6 1.8 fusion.33
  136.4 1.8 fusion.32
  138.2 1.8 fusion.31
  140.1 4.6 %collective-permute-start.3 = (f32[128,1024]{0,1:T(8,128)S(1)}, f32[128,1024]{0,1:T(8,128)S(1)}, u32[]{:S(2)}, u32[]{:S(2)}) collective-permute-start(f32[128,1024]{0,1:T(8,128)S(1)} %get-tuple-element.21), channel_id=1, source_target_pairs={{0,1},{1,2},{2,3},{3,4},{4,5},{5,6},{6,7},{7,8},{8,9},{9,10},{10,1... | collective-permute-start | bytes 1572872 | tf_op jit(solution)/shard_map/ppermute | solution.py:36
  144.7 1.3 collective-permute-start.2
  146.0 21.3 %collective-permute-done.3 = f32[128,1024]{0,1:T(8,128)S(1)} collective-permute-done((f32[128,1024]{0,1:T(8,128)S(1)}, f32[128,1024]{0,1:T(8,128)S(1)}, u32[]{:S(2)}, u32[]{:S(2)}) %collective-permute-start.3) | collective-permute-done | bytes 524320 | tf_op jit(solution)/shard_map/ppermute | solution.py:36
  167.3 0.7 copy-done.1
  168.8 0.7 all-gather.4.cloned.1.call-update
  169.5 1.4 copy.184
  170.9 9.2 %all-to-all-start.1 = ((bf16[16,128,320]{1,2,0:T(8,128)(2,1)}), bf16[16,128,320]{1,2,0:T(8,128)(2,1)S(1)}, u32[]{:S(2)}, u32[]{:S(2)}) async-start(bf16[16,128,320]{1,2,0:T(8,128)(2,1)} %bitcast.65), calls=%async_computation.1 | async-start | bytes 2621440 | tf_op jit(solution)/shard_map/all_to_all | solution.py:135
  180.2 52.2 %all-gather.6.cloned.1.call-done = bf16[2048,512]{0,1:T(8,128)(2,1)} async-done(((bf16[128,512]{0,1:T(8,128)(2,1)}), bf16[2048,512]{0,1:T(8,128)(2,1)}) %all-gather.6.cloned.1.call-update) | async-done | bytes 2097168 | tf_op jit(solution)/shard_map/all_gather | solution.py:142
  232.4 2.9 copy.217
  235.3 1.7 convolution_bitcast_fusion.4
  237.0 2.3 copy.218
  239.4 2.0 fusion.46
  241.5 0.7 fusion.47
  243.1 0.7 fusion.48
  244.7 0.7 fusion.49
  245.5 1.1 copy.186
  246.6 0.8 copy.187
  247.4 50.9 %all-gather.4.cloned.1.call-done = bf16[5120,512]{1,0:T(8,128)(2,1)} async-done(((bf16[320,512]{1,0:T(8,128)(2,1)}), bf16[5120,512]{1,0:T(8,128)(2,1)}) %all-gather.4.cloned.1.call-update) | async-done | bytes 5242896 | tf_op jit(solution)/shard_map/all_gather | solution.py:129
  298.3 5.4 %fusion.4 = bf16[1,128,5120]{2,1,0:T(8,128)(2,1)} fusion(bf16[5120,512]{1,0:T(8,128)(2,1)} %all-gather.4.cloned.1.call-done, bf16[128,1024]{0,1:T(8,128)(2,1)S(1)} %copy-done.2), kind=kOutput, calls=%fused_computation.5 | convolution fusion | flops 671744000 | bytes 6684672 | tf_op jit(solution)/shard_map/dot_general | solution.py:127
  303.6 67.3 %reduce-scatter.4.cloned.1.call-done = f32[32,320]{1,0:T(8,128)} async-done(((f32[512,320]{1,0:T(8,128)}), f32[32,320]{1,0:T(8,128)}) %reduce-scatter.4.cloned.1.call-update) | async-done | bytes 40976
  370.9 0.9 copy.219
  371.9 0.7 copy.188
  (112 shorter events, 8.9 us)
Async XLA Ops:
  11.0 7.6 %copy-start.19 = (s32[1,2048]{1,0:T(1,128)S(1)}, s32[1,2048]{1,0:T(1,128)}, u32[]{:S(2)}) copy-start(s32[1,2048]{1,0:T(1,128)} %param.12) | copy-start | bytes 24580
  11.0 7.7 %copy-start.20 = (s32[1,32]{1,0:T(1,128)S(1)}, s32[1,32]{1,0:T(1,128)}, u32[]{:S(2)}) copy-start(s32[1,32]{1,0:T(1,128)} %param.13) | copy-start | bytes 388
  11.0 83.5 %copy-start = (bf16[1,128,5120]{2,1,0:T(8,128)(2,1)S(1)}, bf16[1,128,5120]{2,1,0:T(8,128)(2,1)}, u32[]{:S(2)}) copy-start(bf16[1,128,5120]{2,1,0:T(8,128)(2,1)} %param.7) | copy-start | bytes 3932164
  11.0 83.5 %all-to-all-start = ((bf16[16,320,512]{2,1,0:T(8,128)(2,1)}), bf16[16,320,512]{2,1,0:T(8,128)(2,1)}, u32[]{:S(2)}, u32[]{:S(2)}) async-start(bf16[16,320,512]{2,1,0:T(8,128)(2,1)} %stack.17), calls=%async_computation | async-start | bytes 10485760 | tf_op jit(solution)/shard_map/all_to_all | solution.py:12
  18.5 213.9 %all-gather.6.cloned.1.call-start = ((), (), s32[]{:S(2)}) async-start(), calls=%async_computation.4 | async-start | bytes 2228224 | tf_op jit(solution)/shard_map/all_gather | solution.py:142
  94.6 3.4 copy-start.6
  94.6 11.2 %copy-start.3 = (bf16[1,128,2560]{2,1,0:T(8,128)(2,1)S(1)}, bf16[1,128,2560]{2,1,0:T(8,128)(2,1)}, u32[]{:S(2)}) copy-start(bf16[1,128,2560]{2,1,0:T(8,128)(2,1)} %param.8) | copy-start | bytes 1966084
  98.0 8.1 %copy-start.4 = (bf16[1,128,2560]{2,1,0:T(8,128)(2,1)S(1)}, bf16[1,128,2560]{2,1,0:T(8,128)(2,1)}, u32[]{:S(2)}) copy-start(bf16[1,128,2560]{2,1,0:T(8,128)(2,1)} %param.10) | copy-start | bytes 1966084
  98.7 10.1 %collective-permute-start.1 = (bf16[128,1024]{1,0:T(8,128)(2,1)}, bf16[128,1024]{1,0:T(8,128)(2,1)}, u32[]{:S(2)}, u32[]{:S(2)}) collective-permute-start(bf16[128,1024]{1,0:T(8,128)(2,1)} %pad_maximum_fusion.2), channel_id=1, source_target_pairs={{1,0},{2,1},{3,2},{4,3},{5,4},{6,5},{7,6},{8,7},{9,8},{10,9},{11,1... | collective-permute-start | bytes 786440 | tf_op jit(solution)/shard_map/ppermute | solution.py:26
  100.0 13.5 %collective-permute-start = (bf16[128,1024]{1,0:T(8,128)(2,1)}, bf16[128,1024]{1,0:T(8,128)(2,1)}, u32[]{:S(2)}, u32[]{:S(2)}) collective-permute-start(bf16[128,1024]{1,0:T(8,128)(2,1)} %pad_maximum_fusion.2), channel_id=1, source_target_pairs={{0,1},{1,2},{2,3},{3,4},{4,5},{5,6},{6,7},{7,8},{8,9},{9,10},{10,1... | collective-permute-start | bytes 786440 | tf_op jit(solution)/shard_map/ppermute | solution.py:24
  116.1 4.4 %copy-start.9 = (bf16[384,1,128]{2,1,0:T(2,128)(2,1)}, bf16[384,1,128]{2,1,0:T(2,128)(2,1)S(1)}, u32[]{:S(2)}) copy-start(bf16[384,1,128]{2,1,0:T(2,128)(2,1)S(1)} %get-tuple-element.26) | copy-start | bytes 294916
  116.1 5.8 %copy-start.7 = (bf16[384,1,128]{2,1,0:T(2,128)(2,1)}, bf16[384,1,128]{2,1,0:T(2,128)(2,1)S(1)}, u32[]{:S(2)}) copy-start(bf16[384,1,128]{2,1,0:T(2,128)(2,1)S(1)} %get-tuple-element.24) | copy-start | bytes 294916
  116.1 1.5 copy-start.13
  116.1 1.5 copy-start.18
  117.6 1.4 copy-start.11
  123.4 1.7 copy-start.21
  125.1 1.1 copy-start.29
  125.1 1.0 copy-start.36
  125.1 1.4 copy-start.5
  125.1 1.5 copy-start.17
  125.1 1.8 copy-start.27
  126.9 1.5 copy-start.25
  127.2 4.8 %copy-start.35 = (f32[5,128,384]{1,2,0:T(8,128)}, f32[5,128,384]{1,2,0:T(8,128)S(1)}, u32[]{:S(2)}) copy-start(f32[5,128,384]{1,2,0:T(8,128)S(1)} %get-tuple-element.37) | copy-start | bytes 2949124
  127.2 4.8 %copy-start.42 = (f32[5,128]{1,0:T(8,128)}, f32[5,128]{1,0:T(8,128)S(1)}, u32[]{:S(2)}) copy-start(f32[5,128]{1,0:T(8,128)S(1)} %get-tuple-element.36) | copy-start | bytes 7684
  128.4 1.5 copy-start.23
  128.7 2.5 copy-start.31
  128.7 2.5 copy-start.38
  130.2 1.0 copy-start.33
  130.2 1.0 copy-start.40
  140.1 27.2 %collective-permute-start.3 = (f32[128,1024]{0,1:T(8,128)S(1)}, f32[128,1024]{0,1:T(8,128)S(1)}, u32[]{:S(2)}, u32[]{:S(2)}) collective-permute-start(f32[128,1024]{0,1:T(8,128)S(1)} %get-tuple-element.21), channel_id=1, source_target_pairs={{0,1},{1,2},{2,3},{3,4},{4,5},{5,6},{6,7},{7,8},{8,9},{9,10},{10,1... | collective-permute-start | bytes 1572872 | tf_op jit(solution)/shard_map/ppermute | solution.py:36
  144.7 22.6 %collective-permute-start.2 = (f32[128,1024]{0,1:T(8,128)S(1)}, f32[128,1024]{0,1:T(8,128)S(1)}, u32[]{:S(2)}, u32[]{:S(2)}) collective-permute-start(f32[128,1024]{0,1:T(8,128)S(1)} %get-tuple-element.20), channel_id=1, source_target_pairs={{1,0},{2,1},{3,2},{4,3},{5,4},{6,5},{7,6},{8,7},{9,8},{10,9},{11,1... | collective-permute-start | bytes 1572872 | tf_op jit(solution)/shard_map/ppermute | solution.py:36
  168.8 129.5 %all-gather.4.cloned.1.call-start = ((), (), s32[]{:S(2)}) async-start(), calls=%async_computation.3 | async-start | bytes 5570560 | tf_op jit(solution)/shard_map/all_gather | solution.py:129
  170.9 64.4 %all-to-all-start.1 = ((bf16[16,128,320]{1,2,0:T(8,128)(2,1)}), bf16[16,128,320]{1,2,0:T(8,128)(2,1)S(1)}, u32[]{:S(2)}, u32[]{:S(2)}) async-start(bf16[16,128,320]{1,2,0:T(8,128)(2,1)} %bitcast.65), calls=%async_computation.1 | async-start | bytes 2621440 | tf_op jit(solution)/shard_map/all_to_all | solution.py:135
  180.1 190.8 %reduce-scatter.4.cloned.1.call-start = ((), (), s32[]{:S(2)}) async-start(), calls=%async_computation.5 | async-start | bytes 835584
  237.0 2.4 copy-start.14
  237.0 2.4 copy-start.28
  237.0 2.4 copy-start.43
  239.4 2.1 copy-start.12
  239.4 2.1 copy-start.26
  239.4 2.1 copy-start.32
  239.4 2.1 copy-start.39
  241.5 1.3 copy-start.24
  241.5 1.6 copy-start.34
  241.5 1.6 copy-start.41
  243.1 1.3 copy-start.22
  243.1 1.6 copy-start.30
  243.1 1.6 copy-start.37
  245.4 52.8 %copy-start.2 = (bf16[128,1024]{0,1:T(8,128)(2,1)S(1)}, bf16[128,1024]{0,1:T(8,128)(2,1)}, u32[]{:S(2)}) copy-start(bf16[128,1024]{0,1:T(8,128)(2,1)} %copy-done.1) | copy-start | bytes 786436
  (5 other events, 4.4 us)
Sparse Core Ops, SparseCore 0:
  168.9 63.5 all-gather.5
  235.2 63.0 all-gather.3
  300.8 70.1 reduce-scatter.3
